TPU v7x, 32 devices: a whole 2x2x4 slice. The times are simulated.
32 devices in a mesh: dp: 8 (over y, x, core), exch: 4 (over z).
Axes of the slice: x: 2, y: 2, z: 4, core: 2. Of those that a mesh axis runs over, the one named last changes fastest.
Arguments:
- x_raw: bfloat16 [1024, 2048], P('exch', 'dp'), may hold values from -6 to 6
- bc_raw: bfloat16 [1024, 256], P(('exch', 'dp')), may hold values from -6 to 6
- dt_raw: bfloat16 [32, 1024], P('dp', 'exch'), may hold values from -4 to 4
- cotangent: bfloat16 [1024, 2048], P('exch', 'dp'), may hold values from -6 to 6
- ssm_state: bfloat16 [8, 32, 64, 128], P('exch', 'dp'), may hold values from -0.625 to 0.625
- conv_x_state: bfloat16 [8, 3, 2048], P('exch', None, 'dp'), may hold values from -6 to 6
- conv_bc_state: bfloat16 [8, 3, 256], P('exch'), may hold values from -6 to 6
- owner: int32 [8], P('exch'), may hold values from 0 to 3, as said below
- resp_len: int32 [8], P('exch'), may hold values from 32 to 128, as said below
- conv_x_weight: float32 [4, 2048], P(None, 'dp'), may hold values from -3 to 3
- conv_bc_weight: float32 [4, 256], replicated, may hold values from -3 to 3
- dt_bias: float32 [32], P('dp'), may hold values from -5 to -3
- a_log: float32 [32], P('dp'), may hold values from -2.3 to 2.1
- skip_d: float32 [32], P('dp'), may hold values from 0.5 to 1.5
Outputs:
- grad_x: bfloat16 [1024, 2048], P('exch', 'dp')
- grad_bc: bfloat16 [1024, 256], P(('exch', 'dp'))
- grad_dt: bfloat16 [32, 1024], P('dp', 'exch')
- grad_conv_x: float32 [4, 2048], P(None, 'dp')
- grad_conv_bc: float32 [4, 256], replicated
- grad_heads: float32 [3, 32], P(None, 'dp')
Inputs may be any that keep to these rules, and one draw needn't show every extreme that they name: `owner`: among the 2 prompts of one holder (an aligned block along exch) no learner index occurs more than 1 times, and some learner index occurs exactly 1 times; over all 8 prompts every learner index occurs exactly 2 times. `resp_len`: every learner's block of 2 responses holds a response of length 128.
All inputs are finite; a program needn't handle non-finite values.
Results may differ from a plain program's by a relative error of at most 0.001.
Values may be sent and summed in bfloat16 or wider, within the bound.
A program may use at most 64 MiB of HBM per device.

v0:
```python
import jax
import jax.numpy as jnp
from jax import lax
from jax.sharding import PartitionSpec as P

DEV_GROUP = 8
SPAN = 128
GROUP = 1
CAP = 1
PRECISE = lax.Precision.HIGHEST


def conv_pre(raw, state, weight):
    padded = jnp.concatenate([state, raw], axis=1)
    length = raw.shape[1]
    total = padded[:, 0:length] * weight[0]
    for offset in range(1, weight.shape[0]):
        total = total + padded[:, offset : offset + length] * weight[offset]
    return total


def ssd_output(values, proj_b, proj_c, steps, rate, skip, start, block):
    rows, length, heads, width = values.shape
    count = length // block
    value_blocks = values.reshape(rows, count, block, heads, width)
    b_blocks = proj_b.reshape(rows, count, block, proj_b.shape[-1])
    c_blocks = proj_c.reshape(rows, count, block, proj_c.shape[-1])
    step_blocks = steps.reshape(rows, count, block, heads)
    logs = jnp.cumsum(-rate * step_blocks, axis=2)
    causal = jnp.tril(jnp.ones((block, block), jnp.float32))
    spread = logs[:, :, :, None, :] - logs[:, :, None, :, :]
    decays = jnp.exp(jnp.where(causal[:, :, None] > 0.5, spread, 0.0)) * causal[:, :, None]
    scores = jnp.einsum("rntk,rnsk->rnts", c_blocks, b_blocks, precision=PRECISE)
    weighted = value_blocks * step_blocks[..., None]
    mixing = scores[..., None] * decays
    intra = jnp.einsum("rntsh,rnshp->rnthp", mixing, weighted, precision=PRECISE)
    entry = jnp.exp(logs[:, 0])
    carried = jnp.einsum("rtk,rhpk->rthp", c_blocks[:, 0], start, precision=PRECISE)
    pieces = [carried * entry[..., None]]
    inter = jnp.stack(pieces, axis=1)
    output = intra + inter + skip[:, None] * value_blocks
    return output.reshape(rows, length, heads, width)


def window_loss(
    x_rows,
    bc_act,
    dt_rows,
    x_weight,
    bias,
    decay_log,
    skip,
    x_prev,
    start,
    cotan,
    mask,
    heads,
    block,
):
    x_act = jax.nn.silu(conv_pre(x_rows, x_prev, x_weight))
    rows, length, channels = x_rows.shape
    values = x_act.reshape(rows, length, heads, channels // heads)
    half = bc_act.shape[-1] // 2
    steps = jax.nn.softplus(dt_rows + bias)
    output = ssd_output(
        values,
        bc_act[..., :half],
        bc_act[..., half:],
        steps,
        jnp.exp(decay_log),
        skip,
        start,
        block,
    )
    return jnp.sum(output.reshape(rows, length, channels) * cotan * mask[..., None])


def local(
    x_raw,
    bc_raw,
    dt_raw,
    cotangent,
    ssm_state,
    conv_x_state,
    conv_bc_state,
    owner,
    resp_len,
    conv_x_weight,
    conv_bc_weight,
    dt_bias,
    a_log,
    skip_d,
):
    peer_count = lax.axis_size("exch")
    slices = lax.axis_size("dp")
    prompts = owner.shape[0]
    responses = resp_len.shape[0]
    head_count = dt_raw.shape[0]
    tokens = x_raw.shape[0]
    channels = x_raw.shape[1]
    pair_width = 2 * ssm_state.shape[-1]
    conv_depth = conv_x_state.shape[1]
    length = tokens // responses
    row_count = bc_raw.shape[0]
    groups = bc_raw.shape[1] // pair_width
    my_group = lax.axis_index("dp") // DEV_GROUP
    targets = jnp.arange(peer_count, dtype=jnp.int32)
    match = (owner[:, None] == targets[None, :]).astype(jnp.int32)
    earlier = jnp.cumsum(match, axis=0) - match
    places = jnp.sum(earlier * match, axis=1)
    slot_ids = jnp.arange(CAP, dtype=jnp.int32)
    routing = (match[:, :, None] == 1) & (places[:, None, None] == slot_ids[None, None, :])
    routing = routing.reshape(prompts, peer_count * CAP).astype(jnp.bfloat16)

    def pack_slots(values):
        moved = jnp.dot(routing.T, values.reshape(prompts, -1), preferred_element_type=jnp.float32)
        return moved.astype(jnp.bfloat16).reshape(peer_count, CAP, -1)

    bc_state = lax.dynamic_slice_in_dim(conv_bc_state, my_group * pair_width, pair_width, 2)
    filled = jnp.sum(routing, axis=0).reshape(peer_count, CAP)
    got_ssm, got_x, got_bc, got_fill = (
        lax.all_to_all(pack_slots(ssm_state), "exch", split_axis=0, concat_axis=0, tiled=True),
        lax.all_to_all(pack_slots(conv_x_state), "exch", split_axis=0, concat_axis=0, tiled=True),
        lax.all_to_all(pack_slots(bc_state), "exch", split_axis=0, concat_axis=0, tiled=True),
        lax.all_to_all(filled, "exch", split_axis=0, concat_axis=0, tiled=True),
    )
    present = (got_fill.reshape(peer_count * CAP) > 0.5).astype(jnp.int32)
    position = jnp.cumsum(present) - 1
    owned_ids = jnp.arange(prompts, dtype=jnp.int32)
    select = ((present[None, :] == 1) & (position[None, :] == owned_ids[:, None])).astype(
        jnp.bfloat16
    )

    def unpack(values, shape):
        chosen = jnp.dot(
            select, values.reshape(peer_count * CAP, -1), preferred_element_type=jnp.float32
        )
        return jnp.repeat(chosen, GROUP, axis=0).reshape(shape)

    start_state = unpack(got_ssm, (responses, head_count, channels // head_count, -1))
    x_prev = unpack(got_x, (responses, conv_depth, channels))
    bc_prev = unpack(got_bc, (responses, conv_depth, pair_width))
    gathered = lax.all_gather(bc_raw, "dp", axis=0, tiled=True)
    bc_local = lax.dynamic_slice_in_dim(gathered, my_group * pair_width, pair_width, 1)
    x_rows = x_raw.astype(jnp.float32).reshape(responses, length, channels)
    bc_rows = bc_local.astype(jnp.float32).reshape(responses, length, pair_width)
    cot_rows = cotangent.astype(jnp.float32).reshape(responses, length, channels)
    dt_rows = dt_raw.astype(jnp.float32).T.reshape(responses, length, head_count)
    live_mask = (jnp.arange(length, dtype=jnp.int32)[None, :] < resp_len[:, None]).astype(
        jnp.float32
    )
    bc_weight = lax.dynamic_slice_in_dim(conv_bc_weight, my_group * pair_width, pair_width, 1)
    bc_pre = conv_pre(bc_rows, bc_prev, bc_weight)
    bc_act, silu_back = jax.vjp(jax.nn.silu, bc_pre)

    def local_loss(x_in, bc_in, dt_in, x_weight, bias, decay_log, skip):
        return window_loss(
            x_in,
            bc_in,
            dt_in,
            x_weight,
            bias,
            decay_log,
            skip,
            x_prev,
            start_state,
            cot_rows,
            live_mask,
            head_count,
            SPAN,
        )

    grad_xr, grad_bca, grad_dtr, grad_wx, grad_bias, grad_decay, grad_skip = jax.grad(
        local_loss, argnums=(0, 1, 2, 3, 4, 5, 6)
    )(x_rows, bc_act, dt_rows, conv_x_weight, dt_bias, a_log, skip_d)
    grad_pre = silu_back(grad_bca)[0]
    unused, conv_back = jax.vjp(
        lambda raw, weight: conv_pre(raw, bc_prev, weight), bc_rows, bc_weight
    )
    grad_raw, grad_wbc = conv_back(grad_pre)
    returned = lax.all_to_all(
        grad_raw.reshape(slices, row_count, pair_width),
        "dp",
        split_axis=0,
        concat_axis=0,
        tiled=True,
    )
    grad_share = jnp.sum(returned.reshape(groups, DEV_GROUP, row_count, pair_width), axis=1)
    grad_share = grad_share.transpose(1, 0, 2).reshape(row_count, groups * pair_width)
    empty_taps = jnp.zeros((conv_depth + 1, groups * pair_width), jnp.float32)
    grad_wx, grad_bias, grad_decay, grad_skip = lax.psum(
        (grad_wx, grad_bias, grad_decay, grad_skip), "exch"
    )
    placed = lax.dynamic_update_slice_in_dim(empty_taps, grad_wbc, my_group * pair_width, 1)
    grad_taps = lax.psum(placed, ("dp", "exch"))
    grad_x = grad_xr.reshape(tokens, channels).astype(jnp.bfloat16)
    grad_bc = grad_share.astype(jnp.bfloat16)
    grad_dt = grad_dtr.reshape(tokens, head_count).T.astype(jnp.bfloat16)
    grad_heads = jnp.stack([grad_bias, grad_decay, grad_skip])
    return (grad_x, grad_bc, grad_dt, grad_wx, grad_taps, grad_heads)


def solution(mesh):
    in_specs = (
        P("exch", "dp"),
        P(("exch", "dp"), None),
        P("dp", "exch"),
        P("exch", "dp"),
        P("exch", "dp", None, None),
        P("exch", None, "dp"),
        P("exch", None, None),
        P("exch"),
        P("exch"),
        P(None, "dp"),
        P(),
        P("dp"),
        P("dp"),
        P("dp"),
    )
    out_specs = (
        P("exch", "dp"),
        P(("exch", "dp"), None),
        P("dp", "exch"),
        P(None, "dp"),
        P(),
        P(None, "dp"),
    )
    return jax.shard_map(local, mesh=mesh, in_specs=in_specs, out_specs=out_specs, check_vma=False)
```

profile of v0, /device:TPU:0, one launch (start us, length us, event | category | flops | bytes accessed | tf_op | source)
XLA Modules:
  0.0 124.4 jit_solution(9123671219750444243)
XLA Ops:
  0.6 0.7 fusion.80
  1.4 0.6 copy-done.8
  2.3 0.7 copy.167
  3.0 6.3 %all-to-all-start = ((bf16[4,1,1]{2,1,0:T(2,128)(2,1)}), bf16[4,1,1]{2,1,0:T(2,128)(2,1)S(1)}, u32[]{:S(2)}, u32[]{:S(2)}) async-start(bf16[4,1,1]{2,1,0:T(2,128)(2,1)} %copy.167), calls=%async_computation | async-start | bytes 4096 | tf_op jit(solution)/shard_map/all_to_all | solution.py:125
  9.4 1.2 reshape.547
  12.8 0.7 copy-done.7
  14.2 0.7 reduce.16
  14.8 0.6 reshape.551
  15.7 0.7 reduce.17
  16.4 0.6 reshape.553
  17.4 0.6 copy-done.4
  18.1 9.3 %all_gather.3 = bf16[256,256]{1,0:T(8,128)(2,1)S(1)} all-gather(bf16[32,256]{1,0:T(8,128)(2,1)S(1)} %copy-done.4), channel_id=1, replica_groups=mesh['dp'=8,'exch'=4] {'dp'}, dimensions={0}, use_global_device_ids=true | all-gather | bytes 147456 | tf_op jit(solution)/shard_map/all_gather | solution.py:143
  27.8 1.0 reduce.18
  28.8 1.0 reshape.555
  29.8 0.9 copy-done.2
  31.1 5.1 %all-to-all-start.1 = ((bf16[4,2,384]{2,1,0:T(2,128)(2,1)}), bf16[4,2,384]{2,1,0:T(2,128)(2,1)S(1)}, u32[]{:S(2)}, u32[]{:S(2)}) async-start(bf16[4,2,384]{2,1,0:T(2,128)(2,1)} %reshape.553), calls=%async_computation.1 | async-start | bytes 12288 | tf_op jit(solution)/shard_map/all_to_all | solution.py:124
  36.6 5.2 %all-to-all-done.1 = bf16[4,2,384]{2,1,0:T(2,128)(2,1)S(1)} async-done(((bf16[4,2,384]{2,1,0:T(2,128)(2,1)}), bf16[4,2,384]{2,1,0:T(2,128)(2,1)S(1)}, u32[]{:S(2)}, u32[]{:S(2)}) %all-to-all-start.1) | async-done | bytes 6176 | tf_op jit(solution)/shard_map/all_to_all | solution.py:124
  41.8 3.2 %all-to-all-start.2 = ((bf16[4,2,384]{2,1,0:T(2,128)(2,1)}), bf16[4,2,384]{2,1,0:T(2,128)(2,1)S(1)}, u32[]{:S(2)}, u32[]{:S(2)}) async-start(bf16[4,2,384]{2,1,0:T(2,128)(2,1)} %reshape.551), calls=%async_computation.2 | async-start | bytes 12288 | tf_op jit(solution)/shard_map/all_to_all | solution.py:123
  45.3 5.4 %all-to-all-done.2 = bf16[4,2,384]{2,1,0:T(2,128)(2,1)S(1)} async-done(((bf16[4,2,384]{2,1,0:T(2,128)(2,1)}), bf16[4,2,384]{2,1,0:T(2,128)(2,1)S(1)}, u32[]{:S(2)}, u32[]{:S(2)}) %all-to-all-start.2) | async-done | bytes 6176 | tf_op jit(solution)/shard_map/all_to_all | solution.py:123
  50.6 3.4 %all-to-all-start.3 = ((bf16[4,2,16384]{2,1,0:T(2,128)(2,1)}), bf16[4,2,16384]{2,1,0:T(2,128)(2,1)S(1)}, u32[]{:S(2)}, u32[]{:S(2)}) async-start(bf16[4,2,16384]{2,1,0:T(2,128)(2,1)} %reshape.555), calls=%async_computation.3 | async-start | bytes 524288 | tf_op jit(solution)/shard_map/all_to_all | solution.py:122
  55.3 1.3 %fusion.10 = (f32[2,128,4]{1,2,0:T(4,128)S(1)}, f32[2,128,4]{1,2,0:T(4,128)S(1)}, f32[2,128,128]{2,1,0:T(8,128)S(1)}) fusion(f32[2,128,128]{2,1,0:T(8,128)S(1)} %fusion.46, f32[128,128]{1,0:T(8,128)S(1)} %fusion.52, f32[2,128,4]{1,2,0:T(4,128)S(1)} %copy.171, pred[128,128]{1,0:T(8,128)(4,1)S(1)} %broadcast_compare_fusion, ...), kind=kOutput, calls=%fused_computation.27 | convolution fusion | flops 102201344 | bytes 885760 | tf_op jit(solution)/shard_map/transpose(jvp(rntsh,rnshp->rnthp))/dot_general | solution.py:36
  56.6 0.7 copy-done.12
  57.3 0.8 multiply_reduce_fusion.10
  59.0 0.7 fusion.19
  62.1 0.6 convolution_bitcast_fusion.2
  63.4 39.4 %psum.36 = f32[4,256]{1,0:T(4,128)} all-reduce(f32[4,256]{1,0:T(4,128)S(1)} %pad_add_fusion.6), channel_id=1, replica_groups=mesh['dp'=8,'exch'=4] {'dp','exch'}, use_global_device_ids=true, to_apply=%region_21.22 | all-reduce | flops 1024 | bytes 8192 | tf_op jit(solution)/shard_map/psum | solution.py:195
  102.9 2.2 %reduce_window_sum.46 = f32[2,1,128,4]{3,2,1,0:T(8,128)S(1)} reduce-window(f32[2,1,128,4]{3,2,1,0:T(8,128)S(1)} %bitcast_add_fusion, f32[]{:T(128)} %constant.56.clone.1), window={size=1x1x128x1 pad=0_0x0_0x0_127x0_0}, to_apply=%region_11.12 | reduce-window | flops 130048 | bytes 8196 | tf_op jit(solution)/shard_map/transpose(jvp(jit(cumsum)))/reduce_window_sum | solution.py:29
  105.2 0.8 multiply_reduce_fusion.11
  106.1 0.8 pad_add_fusion
  106.9 4.8 %all-to-all-start.4 = ((f32[8,32,256]{2,1,0:T(8,128)}), f32[8,32,256]{2,1,0:T(8,128)S(1)}, u32[]{:S(2)}, u32[]{:S(2)}) async-start(f32[8,32,256]{2,1,0:T(8,128)} %bitcast.44), calls=%async_computation.4 | async-start | bytes 524288 | tf_op jit(solution)/shard_map/all_to_all | solution.py:181
  111.9 11.3 %all-reduce.18 = (f32[4,256]{1,0:T(4,128)}, f32[1,4]{1,0:T(1,128)S(1)}, f32[1,4]{1,0:T(1,128)S(1)}, f32[1,4]{1,0:T(1,128)S(1)}) all-reduce(f32[4,256]{1,0:T(4,128)S(1)} %pad_add_fusion.7, f32[1,4]{1,0:T(1,128)S(1)} %bitcast.233, f32[1,4]{1,0:T(1,128)S(1)} %multiply_bitcast_fusion, ...), channel_id=1, replica_groups=mesh['dp'=8,'exch'=4] {'exch'}, use_global_device_ids=true, to_apply=%region_16.17 | all-reduce | flops 1036 | bytes 8288 | tf_op jit(solution)/shard_map/psum | solution.py:191
  123.8 0.6 reduce_sum.196
  (93 shorter events, 11.4 us)
Async XLA Ops:
  0.6 12.8 %copy-start = (bf16[2,3,256]{2,0,1:T(2,128)(2,1)S(1)}, bf16[2,3,256]{2,0,1:T(2,128)(2,1)}, u32[]{:S(2)}) copy-start(bf16[2,3,256]{2,0,1:T(2,128)(2,1)} %param.19) | copy-start | bytes 9220
  1.4 0.7 copy-start.8
  3.0 28.1 %all-to-all-start = ((bf16[4,1,1]{2,1,0:T(2,128)(2,1)}), bf16[4,1,1]{2,1,0:T(2,128)(2,1)S(1)}, u32[]{:S(2)}, u32[]{:S(2)}) async-start(bf16[4,1,1]{2,1,0:T(2,128)(2,1)} %copy.167), calls=%async_computation | async-start | bytes 4096 | tf_op jit(solution)/shard_map/all_to_all | solution.py:125
  9.4 1.2 copy-start.1
  10.6 0.7 copy-start.13
  10.7 0.7 copy-start.11
  11.3 0.7 copy-start.3
  11.3 0.7 copy-start.5
  12.1 0.7 copy-start.6
  12.8 0.7 copy-start.7
  14.8 0.7 copy-start.10
  17.3 0.7 copy-start.4
  18.0 9.4 %copy-start.9 = (bf16[2,4,64,128]{3,2,1,0:T(8,128)(2,1)S(1)}, bf16[2,4,64,128]{3,2,1,0:T(8,128)(2,1)}, u32[]{:S(2)}) copy-start(bf16[2,4,64,128]{3,2,1,0:T(8,128)(2,1)} %param.18) | copy-start | bytes 393220
  29.8 0.9 copy-start.2
  31.1 10.7 %all-to-all-start.1 = ((bf16[4,2,384]{2,1,0:T(2,128)(2,1)}), bf16[4,2,384]{2,1,0:T(2,128)(2,1)S(1)}, u32[]{:S(2)}, u32[]{:S(2)}) async-start(bf16[4,2,384]{2,1,0:T(2,128)(2,1)} %reshape.553), calls=%async_computation.1 | async-start | bytes 12288 | tf_op jit(solution)/shard_map/all_to_all | solution.py:124
  41.8 8.8 %all-to-all-start.2 = ((bf16[4,2,384]{2,1,0:T(2,128)(2,1)}), bf16[4,2,384]{2,1,0:T(2,128)(2,1)S(1)}, u32[]{:S(2)}, u32[]{:S(2)}) async-start(bf16[4,2,384]{2,1,0:T(2,128)(2,1)} %reshape.551), calls=%async_computation.2 | async-start | bytes 12288 | tf_op jit(solution)/shard_map/all_to_all | solution.py:123
  50.6 10.2 %all-to-all-start.3 = ((bf16[4,2,16384]{2,1,0:T(2,128)(2,1)}), bf16[4,2,16384]{2,1,0:T(2,128)(2,1)S(1)}, u32[]{:S(2)}, u32[]{:S(2)}) async-start(bf16[4,2,16384]{2,1,0:T(2,128)(2,1)} %reshape.555), calls=%async_computation.3 | async-start | bytes 524288 | tf_op jit(solution)/shard_map/all_to_all | solution.py:122
  56.6 0.7 copy-start.12
  106.9 16.9 %all-to-all-start.4 = ((f32[8,32,256]{2,1,0:T(8,128)}), f32[8,32,256]{2,1,0:T(8,128)S(1)}, u32[]{:S(2)}, u32[]{:S(2)}) async-start(f32[8,32,256]{2,1,0:T(8,128)} %bitcast.44), calls=%async_computation.4 | async-start | bytes 524288 | tf_op jit(solution)/shard_map/all_to_all | solution.py:181
where the time goes:
time: 125 us; the launch traced here: 124 us
  blocking collectives  60.1 us (48%)
  starting transfers between devices  22.9 us (18%)
  local copies, waits for them, and re-layouts  12.2 us (10%)
  other arithmetic  11.7 us (9%)
  waiting for transfers between devices  11.2 us (9%)
  matrix products  5.42 us (4%)
    psum x1, blocking collectives, local(): grad_taps = lax.psum(placed, ('dp', 'exch'))  39.4 us
    psum x1, blocking collectives, local(): lax.psum((grad_wx, grad_bias, grad_decay, grad_skip), 'exch')  11.3 us
    all_gather x1, blocking collectives, local(): gathered = lax.all_gather(bc_raw, 'dp', axis=0, tiled=True)  9.34 us
    unnamed x37, local copies, waits for them, and re-layouts  7.99 us
    all_to_all x1, starting transfers between devices, local(): lax.all_to_all(filled, 'exch', split_axis=0, concat_axis=0, tiled=True)  6.35 us
    all_to_all x1, waiting for transfers between devices, local(): lax.all_to_all(pack_slots(conv_x_state), 'exch', split_axis=0, concat_axi...  5.35 us
    all_to_all x1, waiting for transfers between devices, local(): lax.all_to_all(pack_slots(bc_state), 'exch', split_axis=0, concat_axis=0,...  5.23 us
    all_to_all x1, starting transfers between devices, local(): lax.all_to_all(pack_slots(bc_state), 'exch', split_axis=0, concat_axis=0,...  5.11 us
  transfers between devices with their start and end apart: 5, of which 3 were waited for; matrix products, arithmetic and copies ran while one was open for 12% of the time, Pallas kernels for 0%

commit v1 on v0

--- a/solution.py
+++ b/solution.py
@@ -8,6 +8,12 @@
 GROUP = 1
 CAP = 1
 PRECISE = lax.Precision.HIGHEST
+
+
+def chunk_extend(my_tile):
+    for p in ("exch", "dp"):
+        my_tile = lax.psum(my_tile, p)
+    return my_tile
 
 
 def conv_pre(raw, state, weight):
@@ -192,7 +198,7 @@
         (grad_wx, grad_bias, grad_decay, grad_skip), "exch"
     )
     placed = lax.dynamic_update_slice_in_dim(empty_taps, grad_wbc, my_group * pair_width, 1)
-    grad_taps = lax.psum(placed, ("dp", "exch"))
+    grad_taps = chunk_extend(placed)
     grad_x = grad_xr.reshape(tokens, channels).astype(jnp.bfloat16)
     grad_bc = grad_share.astype(jnp.bfloat16)
     grad_dt = grad_dtr.reshape(tokens, head_count).T.astype(jnp.bfloat16)

time: 125 us -> 105 us (0.84)
  blocking collectives: 60.1 us -> 35.1 us
  local copies, waits for them, and re-layouts: 12.2 us -> 17.2 us
    psum x1, blocking collectives: 39.4 us -> 12.9 us  [chunk_extend(): my_tile = lax.psum(my_tile, p)]
    unnamed x37 -> x99, local copies, waits for them, and re-layouts: 7.99 us -> 12.4 us
    psum x1, blocking collectives: 11.3 us -> 12.9 us  [local(): lax.psum((grad_wx, grad_bias, grad_decay, grad_skip), 'exch')]
    all_to_all x1, starting transfers between devices: 4.78 us -> 3.41 us  [local(): lax.all_to_all(grad_raw.reshape(slices, row_count, pair_width), 'dp', spl...]
  transfers between devices with their start and end apart: 5 -> 5, of which waited for: 3 -> 2; matrix products, arithmetic and copies ran while one was open for 12% -> 16% of each run, Pallas kernels for 0% -> 0%
where the time goes in v1:
time: 105 us; the launch traced here: 104 us
  blocking collectives  35.1 us (33%)
  starting transfers between devices  21.7 us (21%)
  local copies, waits for them, and re-layouts  17.2 us (16%)
  other arithmetic  12.2 us (12%)
  waiting for transfers between devices  10.6 us (10%)
  matrix products  5.99 us (6%)
  between operations  1.3 us (1%)
    psum x1, blocking collectives, chunk_extend(): my_tile = lax.psum(my_tile, p)  12.9 us
    psum x1, blocking collectives, local(): lax.psum((grad_wx, grad_bias, grad_decay, grad_skip), 'exch')  12.9 us
    unnamed x99, local copies, waits for them, and re-layouts  12.4 us
    all_gather x1, blocking collectives, local(): gathered = lax.all_gather(bc_raw, 'dp', axis=0, tiled=True)  9.34 us
    all_to_all x1, starting transfers between devices, local(): lax.all_to_all(filled, 'exch', split_axis=0, concat_axis=0, tiled=True)  6.35 us
    all_to_all x1, waiting for transfers between devices, local(): lax.all_to_all(pack_slots(conv_x_state), 'exch', split_axis=0, concat_axi...  5.35 us
    all_to_all x1, waiting for transfers between devices, local(): lax.all_to_all(pack_slots(bc_state), 'exch', split_axis=0, concat_axis=0,...  5.23 us
    all_to_all x1, starting transfers between devices, local(): lax.all_to_all(pack_slots(bc_state), 'exch', split_axis=0, concat_axis=0,...  5.1 us
  transfers between devices with their start and end apart: 5, of which 2 were waited for; matrix products, arithmetic and copies ran while one was open for 16% of the time, Pallas kernels for 0%

profile of v1, /device:TPU:0, one launch (start us, length us, event | category | flops | bytes accessed | tf_op | source)
XLA Modules:
  0.0 104.1 jit_solution(4896721034220120818)
XLA Ops:
  0.6 0.7 fusion.80
  2.3 0.7 copy.167
  3.0 6.3 %all-to-all-start = ((bf16[4,1,1]{2,1,0:T(2,128)(2,1)}), bf16[4,1,1]{2,1,0:T(2,128)(2,1)S(1)}, u32[]{:S(2)}, u32[]{:S(2)}) async-start(bf16[4,1,1]{2,1,0:T(2,128)(2,1)} %copy.167), calls=%async_computation | async-start | bytes 4096 | tf_op jit(solution)/shard_map/all_to_all | solution.py:131
  9.4 1.2 %reshape.547 = f32[2,1,128,4,64]{4,3,2,0,1:T(4,128)S(1)} reshape(bf16[256,256]{1,0:T(8,128)(2,1)} %param.17) | data formatting | bytes 393216 | tf_op jit(solution)/shard_map/reshape | solution.py:153
  12.8 0.7 copy-done.31
  14.2 0.7 reduce.16
  15.8 0.7 reduce.17
  18.1 9.3 %all_gather.3 = bf16[256,256]{1,0:T(8,128)(2,1)S(1)} all-gather(bf16[32,256]{1,0:T(8,128)(2,1)S(1)} %copy-done.9), channel_id=1, replica_groups=mesh['dp'=8,'exch'=4] {'dp'}, dimensions={0}, use_global_device_ids=true | all-gather | bytes 147456 | tf_op jit(solution)/shard_map/all_gather | solution.py:149
  27.5 0.7 copy.179
  28.5 1.0 reduce.18
  29.5 1.0 reshape.555
  30.5 0.9 copy-done.2
  31.8 5.1 %all-to-all-start.1 = ((bf16[4,2,384]{2,1,0:T(2,128)(2,1)}), bf16[4,2,384]{2,1,0:T(2,128)(2,1)S(1)}, u32[]{:S(2)}, u32[]{:S(2)}) async-start(bf16[4,2,384]{2,1,0:T(2,128)(2,1)} %reshape.553), calls=%async_computation.1 | async-start | bytes 12288 | tf_op jit(solution)/shard_map/all_to_all | solution.py:130
  37.2 5.2 %all-to-all-done.1 = bf16[4,2,384]{2,1,0:T(2,128)(2,1)S(1)} async-done(((bf16[4,2,384]{2,1,0:T(2,128)(2,1)}), bf16[4,2,384]{2,1,0:T(2,128)(2,1)S(1)}, u32[]{:S(2)}, u32[]{:S(2)}) %all-to-all-start.1) | async-done | bytes 6176 | tf_op jit(solution)/shard_map/all_to_all | solution.py:130
  42.5 3.2 %all-to-all-start.2 = ((bf16[4,2,384]{2,1,0:T(2,128)(2,1)}), bf16[4,2,384]{2,1,0:T(2,128)(2,1)S(1)}, u32[]{:S(2)}, u32[]{:S(2)}) async-start(bf16[4,2,384]{2,1,0:T(2,128)(2,1)} %reshape.551), calls=%async_computation.2 | async-start | bytes 12288 | tf_op jit(solution)/shard_map/all_to_all | solution.py:129
  45.9 5.3 %all-to-all-done.2 = bf16[4,2,384]{2,1,0:T(2,128)(2,1)S(1)} async-done(((bf16[4,2,384]{2,1,0:T(2,128)(2,1)}), bf16[4,2,384]{2,1,0:T(2,128)(2,1)S(1)}, u32[]{:S(2)}, u32[]{:S(2)}) %all-to-all-start.2) | async-done | bytes 6176 | tf_op jit(solution)/shard_map/all_to_all | solution.py:129
  51.3 3.6 %all-to-all-start.3 = ((bf16[4,2,16384]{2,1,0:T(2,128)(2,1)}), bf16[4,2,16384]{2,1,0:T(2,128)(2,1)S(1)}, u32[]{:S(2)}, u32[]{:S(2)}) async-start(bf16[4,2,16384]{2,1,0:T(2,128)(2,1)} %reshape.555), calls=%async_computation.3 | async-start | bytes 524288 | tf_op jit(solution)/shard_map/all_to_all | solution.py:128
  55.2 0.8 multiply_reduce_fusion.1
  57.5 1.4 %multiply_reduce_fusion.10 = (f32[2,128,4]{1,2,0:T(4,128)}, f32[2,1,128,4,64]{2,4,3,0,1:T(8,128)S(1)}) fusion(f32[2,1,128,4,64]{2,4,3,0,1:T(8,128)S(1)} %bitcast.201, f32[2,128,4]{1,2,0:T(4,128)S(1)} %compare_select_fusion.5, f32[2,1,128,4,64]{2,4,3,0,1:T(8,128)S(1)} %copy.166, f32[2,128]{1,0:T(2,128)S(1)} %compare_convert_fusion.1, f32[4]{0:T(128)S(1)} %copy-done.42, ...), kind=kOutput, calls=%fused_computation.60 | convolution fusion | flops 101645312 | bytes 1012752 | tf_op jit(solution)/shard_map/transpose(jvp(rntsh,rnshp->rnthp))/dot_general | solution.py:42
  59.4 0.7 copy-done.4
  60.1 1.3 %fusion.10 = (f32[2,128,4]{1,2,0:T(4,128)S(1)}, f32[2,128,4]{1,2,0:T(4,128)S(1)}, f32[2,128,128]{2,1,0:T(8,128)S(1)}) fusion(f32[2,128,128]{2,1,0:T(8,128)S(1)} %copy-done.4, f32[128,128]{1,0:T(8,128)S(1)} %copy-done.6, f32[2,128,4]{1,2,0:T(4,128)S(1)} %copy-done.29, pred[128,128]{1,0:T(8,128)(4,1)S(1)} %copy-done.12, f32[2,128,4,64]{1,3,2,0:T(8,128)S(1)} %bitcast.202, ...), kind=kOutput, calls=%fused_computation.27 | convolution fusion | flops 102201344 | bytes 885760 | tf_op jit(solution)/shard_map/transpose(jvp(rntsh,rnshp->rnthp))/dot_general | solution.py:42
  61.4 0.7 copy-done.27
  62.6 0.7 fusion.19
  64.4 0.7 copy-done.36
  66.0 0.6 convolution_bitcast_fusion.2
  67.2 2.2 %reduce_window_sum.46 = f32[2,1,128,4]{3,2,1,0:T(8,128)S(1)} reduce-window(f32[2,1,128,4]{3,2,1,0:T(8,128)S(1)} %bitcast_add_fusion, f32[]{:T(128)} %constant.56.clone.1), window={size=1x1x128x1 pad=0_0x0_0x0_127x0_0}, to_apply=%region_11.12 | reduce-window | flops 130048 | bytes 8196 | tf_op jit(solution)/shard_map/transpose(jvp(jit(cumsum)))/reduce_window_sum | solution.py:35
  70.2 0.8 multiply_reduce_fusion.11
  71.0 0.7 copy-done.44
  72.9 0.8 pad_add_fusion
  73.6 3.4 %all-to-all-start.4 = ((f32[8,32,256]{2,1,0:T(8,128)}), f32[8,32,256]{2,1,0:T(8,128)S(1)}, u32[]{:S(2)}, u32[]{:S(2)}) async-start(f32[8,32,256]{2,1,0:T(8,128)} %bitcast.44), calls=%async_computation.4 | async-start | bytes 524288 | tf_op jit(solution)/shard_map/all_to_all | solution.py:187
  77.1 12.9 %all-reduce.18 = (f32[4,256]{1,0:T(4,128)}, f32[4,256]{1,0:T(4,128)S(1)}, f32[1,4]{1,0:T(1,128)S(1)}, f32[1,4]{1,0:T(1,128)S(1)}, f32[1,4]{1,0:T(1,128)S(1)}) all-reduce(f32[4,256]{1,0:T(4,128)S(1)} %get-tuple-element.51, f32[4,256]{1,0:T(4,128)S(1)} %get-tuple-element.50, ...), channel_id=1, replica_groups=mesh['dp'=8,'exch'=4] {'exch'}, use_global_device_ids=true, to_apply=%region_16.17 | all-reduce | flops 2060 | bytes 16480 | tf_op jit(solution)/shard_map/psum | solution.py:197
  90.0 12.9 %psum.44 = f32[4,256]{1,0:T(4,128)} all-reduce(f32[4,256]{1,0:T(4,128)S(1)} %get-tuple-element.18), channel_id=1, replica_groups=mesh['dp'=8,'exch'=4] {'dp'}, use_global_device_ids=true, to_apply=%region_22.23 | all-reduce | flops 1024 | bytes 8192 | tf_op jit(solution)/shard_map/psum | solution.py:15
  (154 shorter events, 15.9 us)
Async XLA Ops:
  0.6 12.9 %copy-start = (bf16[2,3,256]{2,0,1:T(2,128)(2,1)S(1)}, bf16[2,3,256]{2,0,1:T(2,128)(2,1)}, u32[]{:S(2)}) copy-start(bf16[2,3,256]{2,0,1:T(2,128)(2,1)} %param.19) | copy-start | bytes 9220
  3.0 28.8 %all-to-all-start = ((bf16[4,1,1]{2,1,0:T(2,128)(2,1)}), bf16[4,1,1]{2,1,0:T(2,128)(2,1)S(1)}, u32[]{:S(2)}, u32[]{:S(2)}) async-start(bf16[4,1,1]{2,1,0:T(2,128)(2,1)} %copy.167), calls=%async_computation | async-start | bytes 4096 | tf_op jit(solution)/shard_map/all_to_all | solution.py:131
  9.4 47.4 %copy-start.11 = (pred[128,128]{1,0:T(8,128)(4,1)}, pred[128,128]{1,0:T(8,128)(4,1)S(1)}, u32[]{:S(2)}) copy-start(pred[128,128]{1,0:T(8,128)(4,1)S(1)} %broadcast_compare_fusion) | copy-start | bytes 49156
  9.4 47.4 %copy-start.5 = (f32[128,128]{1,0:T(8,128)}, f32[128,128]{1,0:T(8,128)S(1)}, u32[]{:S(2)}) copy-start(f32[128,128]{1,0:T(8,128)S(1)} %fusion.52) | copy-start | bytes 196612
  9.4 1.2 %copy-start.1 = (bf16[256,256]{1,0:T(8,128)(2,1)S(1)}, bf16[256,256]{1,0:T(8,128)(2,1)}, u32[]{:S(2)}) copy-start(bf16[256,256]{1,0:T(8,128)(2,1)} %param.17) | copy-start | bytes 393220
  11.3 0.8 copy-start.25
  12.0 44.8 %copy-start.13 = (f32[2,128]{1,0:T(2,128)}, f32[2,128]{1,0:T(2,128)S(1)}, u32[]{:S(2)}) copy-start(f32[2,128]{1,0:T(2,128)S(1)} %compare_convert_fusion.1) | copy-start | bytes 3076
  12.1 44.7 %copy-start.32 = (f32[2,128,4]{1,2,0:T(4,128)}, f32[2,128,4]{1,2,0:T(4,128)S(1)}, u32[]{:S(2)}) copy-start(f32[2,128,4]{1,2,0:T(4,128)S(1)} %compare_select_fusion.5) | copy-start | bytes 12292
  12.1 0.7 copy-start.30
  13.5 42.7 %copy-start.15 = (f32[1,256]{1,0:T(1,128)}, f32[1,256]{1,0:T(1,128)S(1)}, u32[]{:S(2)}) copy-start(f32[1,256]{1,0:T(1,128)S(1)} %get-tuple-element.42) | copy-start | bytes 3076
  13.5 42.7 %copy-start.17 = (f32[1,256]{1,0:T(1,128)}, f32[1,256]{1,0:T(1,128)S(1)}, u32[]{:S(2)}) copy-start(f32[1,256]{1,0:T(1,128)S(1)} %get-tuple-element.43) | copy-start | bytes 3076
  13.5 42.7 %copy-start.19 = (f32[1,256]{1,0:T(1,128)}, f32[1,256]{1,0:T(1,128)S(1)}, u32[]{:S(2)}) copy-start(f32[1,256]{1,0:T(1,128)S(1)} %get-tuple-element.44) | copy-start | bytes 3076
  13.5 42.7 %copy-start.21 = (f32[1,256]{1,0:T(1,128)}, f32[1,256]{1,0:T(1,128)S(1)}, u32[]{:S(2)}) copy-start(f32[1,256]{1,0:T(1,128)S(1)} %get-tuple-element.45) | copy-start | bytes 3076
  14.9 0.7 copy-start.40
  17.4 0.7 copy-start.9
  18.1 38.7 %copy-start.28 = (f32[2,128,4]{1,2,0:T(4,128)}, f32[2,128,4]{1,2,0:T(4,128)S(1)}, u32[]{:S(2)}) copy-start(f32[2,128,4]{1,2,0:T(4,128)S(1)} %copy.171) | copy-start | bytes 12292
  18.1 10.0 %copy-start.39 = (bf16[2,4,64,128]{3,2,1,0:T(8,128)(2,1)S(1)}, bf16[2,4,64,128]{3,2,1,0:T(8,128)(2,1)}, u32[]{:S(2)}) copy-start(bf16[2,4,64,128]{3,2,1,0:T(8,128)(2,1)} %param.18) | copy-start | bytes 393220
  30.5 0.9 copy-start.2
  31.8 10.7 %all-to-all-start.1 = ((bf16[4,2,384]{2,1,0:T(2,128)(2,1)}), bf16[4,2,384]{2,1,0:T(2,128)(2,1)S(1)}, u32[]{:S(2)}, u32[]{:S(2)}) async-start(bf16[4,2,384]{2,1,0:T(2,128)(2,1)} %reshape.553), calls=%async_computation.1 | async-start | bytes 12288 | tf_op jit(solution)/shard_map/all_to_all | solution.py:130
  37.2 17.8 %copy-start.37 = (s32[4]{0:T(128)}, s32[4]{0:T(128)S(1)}, u32[]{:S(2)}) copy-start(s32[4]{0:T(128)S(1)} %add_bitcast_fusion) | copy-start | bytes 52
  42.5 8.8 %all-to-all-start.2 = ((bf16[4,2,384]{2,1,0:T(2,128)(2,1)}), bf16[4,2,384]{2,1,0:T(2,128)(2,1)S(1)}, u32[]{:S(2)}, u32[]{:S(2)}) async-start(bf16[4,2,384]{2,1,0:T(2,128)(2,1)} %reshape.551), calls=%async_computation.2 | async-start | bytes 12288 | tf_op jit(solution)/shard_map/all_to_all | solution.py:129
  45.9 9.1 %copy-start.35 = (pred[4]{0:T(512)(128)(4,1)}, pred[4]{0:T(512)(128)(4,1)S(1)}, u32[]{:S(2)}) copy-start(pred[4]{0:T(512)(128)(4,1)S(1)} %compare_reduce_fusion) | copy-start | bytes 16
  51.3 12.5 %all-to-all-start.3 = ((bf16[4,2,16384]{2,1,0:T(2,128)(2,1)}), bf16[4,2,16384]{2,1,0:T(2,128)(2,1)S(1)}, u32[]{:S(2)}, u32[]{:S(2)}) async-start(bf16[4,2,16384]{2,1,0:T(2,128)(2,1)} %reshape.555), calls=%async_computation.3 | async-start | bytes 524288 | tf_op jit(solution)/shard_map/all_to_all | solution.py:128
  56.8 2.1 %copy-start.3 = (f32[2,128,128]{2,1,0:T(8,128)}, f32[2,128,128]{2,1,0:T(8,128)S(1)}, u32[]{:S(2)}) copy-start(f32[2,128,128]{2,1,0:T(8,128)S(1)} %fusion.46) | copy-start | bytes 393220
  59.2 0.9 copy-start.4
  59.2 0.9 copy-start.6
  59.2 0.9 copy-start.12
  59.3 0.9 copy-start.29
  59.3 0.9 copy-start.33
  59.4 0.8 copy-start.14
  69.4 0.7 copy-start.10
  73.6 29.8 %all-to-all-start.4 = ((f32[8,32,256]{2,1,0:T(8,128)}), f32[8,32,256]{2,1,0:T(8,128)S(1)}, u32[]{:S(2)}, u32[]{:S(2)}) async-start(f32[8,32,256]{2,1,0:T(8,128)} %bitcast.44), calls=%async_computation.4 | async-start | bytes 524288 | tf_op jit(solution)/shard_map/all_to_all | solution.py:187
  (18 other events, 12.0 us)
